TPU v7x, 32 devices: a whole 2x2x4 slice. The times are simulated.
32 devices in a mesh: sample: 2 (over x), space: 16 (over z, y, core).
Axes of the slice: x: 2, y: 2, z: 4, core: 2. Of those that a mesh axis runs over, the one named last changes fastest.
Arguments:
- volume: bfloat16 [2, 128, 16, 1024], P('sample', 'space'), may hold values from -6 to 6
- cotangent: bfloat16 [2, 16, 2, 4, 256], P('sample', 'space'), may hold values from -0.375 to 0.375
- weight_first: bfloat16 [3, 3, 3, 32, 64], replicated, may hold values from -0.21875 to 0.21875
- weight_mid: bfloat16 [3, 3, 3, 64, 128], replicated, may hold values from -0.15625 to 0.15625
- weight_last: bfloat16 [3, 3, 3, 128, 256], P(None, None, None, None, 'sample'), may hold values from -0.109375 to 0.109375
Outputs:
- out_act: bfloat16 [2, 16, 2, 4, 256], P('sample', 'space')
- grad_first: float32 [3, 3, 3, 32, 64], replicated
- grad_mid: float32 [3, 3, 3, 64, 128], replicated
- grad_last: float32 [3, 3, 3, 128, 256], P(None, None, None, None, 'sample')
All inputs are finite; a program needn't handle non-finite values.
Results may differ from a plain program's by a relative error of at most 0.015.
The roundings to bfloat16 on the way count: a program that leaves them out, or rounds other values in their place, can miss the bound.
Values may be sent and summed in bfloat16 or wider, within the bound.
A program may use at most 128 MiB of HBM per device.

v0:
```python
import functools

import jax
import jax.numpy as jnp
from jax import lax
from jax.experimental import pallas as pl
from jax.experimental.pallas import tpu as pltpu
from jax.sharding import PartitionSpec as P

LEAK = 0.3


def leak_relu(value):
    return jnp.where(value > 0, value, LEAK * value)


def leak_slope(value):
    return jnp.where(value > 0, jnp.float32(1.0), jnp.float32(LEAK))


def shift_up(field):
    rows = field.shape[2]
    rolled = pltpu.roll(field.reshape(-1, rows, 128), 1, 1)
    keep = lax.broadcasted_iota(jnp.int32, rolled.shape, 1) > 0
    return jnp.where(keep, rolled, 0.0).reshape(field.shape)


def shift_down(field):
    rows = field.shape[2]
    rolled = pltpu.roll(field.reshape(-1, rows, 128), rows - 1, 1)
    keep = lax.broadcasted_iota(jnp.int32, rolled.shape, 1) < rows - 1
    return jnp.where(keep, rolled, 0.0).reshape(field.shape)


def tap_rows(field, rim):
    size_x, size_y, groups, lanes = field.shape
    split = field.reshape(size_x // 2, 2, size_y, groups, lanes)
    odd_x = jnp.concatenate([rim[None], split[:, 1]], axis=0)
    planes = (odd_x[:-1], split[:, 0], odd_x[1:])
    taps = []
    for plane in planes:
        count = plane.shape[0]
        parts = plane.reshape(count, size_y // 2, 2, groups, lanes)
        zero = jnp.zeros((count, 1, groups, lanes), field.dtype)
        odd_y = jnp.concatenate([zero, parts[:, :, 1]], axis=1)
        for piece in (odd_y[:, :-1], parts[:, :, 0], odd_y[:, 1:]):
            wide = jnp.concatenate([shift_up(piece), piece], axis=3)
            taps.append(wide.reshape(-1, 2 * lanes).astype(jnp.bfloat16))
    return taps


def conv_taps(taps, wide):
    total = None
    for tap, rows in enumerate(taps):
        part = jnp.dot(rows, wide[tap], preferred_element_type=jnp.float32)
        total = part if total is None else total + part
    return total


def spread_back(grad, wide, out_x, out_y, groups):
    planes = []
    for tap_x in range(3):
        pieces = []
        for tap_y in range(3):
            part = lax.dot_general(
                grad, wide[3 * tap_x + tap_y], (((1,), (1,)), ((), ())), preferred_element_type=jnp.float32
            )
            part = part.reshape(out_x, out_y, groups, 256)
            pieces.append(shift_down(part[..., :128]) + part[..., 128:])
        zero = jnp.zeros((out_x, 1, groups, 128), jnp.float32)
        odd_y = pieces[2] + jnp.concatenate([pieces[0][:, 1:], zero], axis=1)
        whole = jnp.concatenate([pieces[1][:, :, None], odd_y[:, :, None]], axis=2)
        planes.append(whole.reshape(out_x, 2 * out_y, groups, 128))
    zero = jnp.zeros((1,) + planes[0].shape[1:], jnp.float32)
    odd_x = planes[2] + jnp.concatenate([planes[0][1:], zero], axis=0)
    field = jnp.concatenate([planes[1][:, None], odd_x[:, None]], axis=1)
    return planes[0][0], field.reshape(2 * out_x, 2 * out_y, groups, 128)


def contract_rows(rows, grad):
    return lax.dot_general(rows, grad, (((0,), (0,)), ((), ())), preferred_element_type=jnp.float32)


MESH = pl.DeviceIdType.MESH
VM = pl.BlockSpec(memory_space=pltpu.VMEM)
BLOCK = 80


def roll_rows(tile, by):
    flat = tile.reshape(-1, 8, 128)
    return pltpu.roll(flat, by, 1).reshape(tile.shape)


def row_of(tile):
    return lax.broadcasted_iota(jnp.int32, tile.shape, tile.ndim - 2)


def last_taps(acts, before):
    count = acts.shape[0]
    planes = []
    for field in (acts, before):
        even = field[:, :32].reshape(count, 2, 2, 8, 128)
        odd = field[:, 32:64].reshape(count, 2, 2, 8, 128)
        moved = roll_rows(odd, 1)
        moved = jnp.where(lax.rem(row_of(moved), 4) > 0, moved, 0.0)
        planes.append((moved, even, odd))
    taps = []
    for tap_x in range(3):
        for tap_y in range(3):
            for tap_z in range(3):
                tiles = planes[1 if tap_x == 0 else 0][tap_z][:, 0 if tap_x == 1 else 1]
                low, high = tiles[:, 0], tiles[:, 1]
                upper = row_of(low) < 4
                if tap_y == 0:
                    rows = jnp.where(upper, 0.0, low)
                elif tap_y == 1:
                    rows = jnp.where(upper, low, roll_rows(high, 4))
                else:
                    rows = jnp.where(upper, roll_rows(low, 4), high)
                taps.append(rows.reshape(count * 8, 128).astype(jnp.bfloat16))
    return taps


def last_back(cots, weight_last, samples):
    flat = cots.reshape(samples * 16, -1)

    def part(tap_x, tap_y, tap_z):
        value = lax.dot_general(
            flat,
            weight_last[9 * tap_x + 3 * tap_y + tap_z],
            (((1,), (1,)), ((), ())),
            preferred_element_type=jnp.float32,
        )
        return value.reshape(samples, 2, 8, 128)

    tiles = ([], [])
    for plane in range(2):
        rows = [[None] * 3 for _ in range(3)]
        for tap_y in range(3):
            for tap_z in range(3):
                if plane == 0:
                    rows[tap_y][tap_z] = part(1, tap_y, tap_z)[:, 0]
                else:
                    rows[tap_y][tap_z] = part(2, tap_y, tap_z)[:, 0] + part(0, tap_y, tap_z)[:, 1]
        for parity in range(2):
            picked = []
            for tap_y in range(3):
                if parity == 0:
                    picked.append(rows[tap_y][1])
                else:
                    moved = roll_rows(rows[tap_y][0], 7)
                    moved = jnp.where(lax.rem(row_of(moved), 4) < 3, moved, 0.0)
                    picked.append(rows[tap_y][2] + moved)
            upper = row_of(picked[0]) < 4
            tiles[parity].append(jnp.where(upper, picked[1], roll_rows(picked[2], 4) + picked[0]))
            tiles[parity].append(jnp.where(upper, roll_rows(picked[1], 4), picked[2]))
    return jnp.concatenate(tiles[0] + tiles[1], axis=1)


def whole_kernel(
    samples, spaces, dims, rows_each,
    volume, cotangent, weight_first, weight_mid, weight_last,
    out_act, result, grad_last,
    cells, rim_cells, half_sem, last_sem, rim, act_send, act_rim, back_send, back_rim,
    cot_in, dact_send, dact_in, mid_rows, block, blocks,
    data, half_in, mine, parts, done, out_send, out_in,
    ring, cot_sem, swap, send, recv, pair_sem, gather_send, gather_recv, out_sem,
):
    size_x, size_y, groups = dims
    sample = lax.axis_index("sample")
    space = lax.axis_index("space")
    core = lax.rem(space, 2)
    pairs = spaces // 2
    chips = samples * pairs
    chip = sample * pairs + space // 2
    filters = weight_last.shape[2]

    def at(by_sample, by_space):
        return {
            "sample": lax.rem(sample + by_sample, samples),
            "space": lax.rem(space + by_space + spaces, spaces),
        }

    def peer(to):
        return {"sample": to // pairs, "space": lax.rem(to, pairs) * 2 + core}

    partner = {"sample": sample, "space": space + 1 - 2 * core}
    barrier = pltpu.get_barrier_semaphore()
    near = [partner] + [at(by, step) for by in range(samples) for step in (1, -1)]
    for device in near:
        pl.semaphore_signal(barrier, inc=1, device_id=device, device_id_type=MESH)

    def tell(step, carry):
        pl.semaphore_signal(
            barrier, inc=1, device_id=peer(lax.rem(chip + step, chips)), device_id_type=MESH
        )
        return carry

    lax.fori_loop(1, chips, tell, 0)
    pl.semaphore_wait(barrier, chips - 1 + len(near))

    def link(source, target, sems, slot, device):
        return pltpu.make_async_remote_copy(
            src_ref=source,
            dst_ref=target,
            send_sem=sems.at[2 * slot],
            recv_sem=sems.at[2 * slot + 1],
            device_id=device,
            device_id_type=MESH,
        )

    cot_copies = []
    for by in range(samples):
        for ahead in range(2):
            if by or ahead:
                slot = 2 * by + ahead
                cot_copies.append(
                    link(cotangent, cot_in.at[ahead, by], cot_sem, slot, at(by, -ahead))
                )
                cot_copies[-1].start()
    first = link(volume.at[pl.ds((size_x - 1) * size_y, size_y)], rim, ring, 0, at(0, 1))
    first.start()

    def pick(value):
        kept = value[..., :filters]
        for shard in range(1, samples):
            kept = jnp.where(sample == shard, value[..., shard * filters : (shard + 1) * filters], kept)
        return kept

    def cells_of(value):
        wide = value.astype(jnp.float32)
        return jnp.concatenate([wide[0], wide[1]], axis=0)

    own_cot = cells_of(cotangent[...])
    block[64:80] = jnp.concatenate([own_cot[:, :128], own_cot[:, 128:]], axis=0).astype(jnp.bfloat16)
    for group in range(groups):
        lanes = volume[:, 128 * group : 128 * group + 128].astype(jnp.float32)
        cells[pl.ds(group, size_x * size_y, stride=groups), :] = lanes
    flat_first = weight_first[...].astype(jnp.float32)
    wide_first, wide_mid = [], []
    for tap in range(9):
        piece = flat_first[96 * tap : 96 * tap + 96]
        gap = jnp.zeros((96, 64), jnp.float32)
        left = jnp.concatenate([gap, piece, gap[:64]], axis=0)
        right = jnp.concatenate([gap, gap[:64], piece], axis=0)
        wide_first.append(jnp.concatenate([left, right], axis=1).astype(jnp.bfloat16))
        piece = weight_mid[192 * tap : 192 * tap + 192]
        wide_mid.append(jnp.concatenate([jnp.zeros((64, 128), jnp.bfloat16), piece], axis=0))

    for copy in cot_copies:
        copy.wait()
    cots = []
    for by in range(samples):
        own = own_cot if by == 0 else cells_of(cot_in[0, by])
        nxt = jnp.where(space < spaces - 1, cells_of(cot_in[1, by]), 0.0)
        cots.append(pick(own))
        cots.append(pick(nxt))
    cots = jnp.concatenate(cots, axis=0).astype(jnp.bfloat16)
    dact_send[...] = last_back(cots, weight_last, samples).astype(jnp.bfloat16)
    swaps = []
    for by in range(1, samples):
        swaps.append(link(dact_send.at[by], dact_in.at[by], swap, by, at(samples - by, 0)))
        swaps[-1].start()

    first.wait()
    field = cells[...].reshape(size_x, size_y, groups, 128)
    for group in range(groups):
        lanes = rim[:, 128 * group : 128 * group + 128].astype(jnp.float32)
        rim_cells[pl.ds(group, size_y, stride=groups), :] = jnp.where(space > 0, lanes, 0.0)
    edge = rim_cells[...].reshape(size_y, groups, 128)
    taps_first = tap_rows(field, edge)
    pre_first = conv_taps(taps_first, wide_first)
    act_first = leak_relu(pre_first).astype(jnp.bfloat16)
    half = (size_x // 2, size_y // 2)
    side = half[1] * groups
    act_send[...] = act_first[-side:]
    second = link(act_send, act_rim, ring, 1, at(0, 1))
    second.start()
    second.wait()
    edge = jnp.where(space > 0, act_rim[...].astype(jnp.float32), 0.0).reshape(half[1], groups, 128)
    taps_mid = tap_rows(act_first.astype(jnp.float32).reshape(half + (groups, 128)), edge)
    pre_mid = conv_taps(taps_mid, wide_mid)
    mid_rows[...] = leak_relu(pre_mid).astype(jnp.bfloat16).astype(jnp.float32)
    block[:32] = mid_rows[pl.ds(0, 32, stride=2), :].astype(jnp.bfloat16)
    block[32:64] = mid_rows[pl.ds(1, 32, stride=2), :].astype(jnp.bfloat16)

    def gather(step, slot):
        return pltpu.make_async_remote_copy(
            src_ref=block,
            dst_ref=blocks.at[slot, core],
            send_sem=gather_send.at[step],
            recv_sem=gather_recv.at[step],
            device_id=peer(lax.rem(chip + step, chips)),
            device_id_type=MESH,
        )

    def start_gather(step, carry):
        gather(step, chip).start()
        return carry

    def wait_gather(step, carry):
        gather(step, lax.rem(chip + chips - step, chips)).wait()
        return carry

    for copy in swaps:
        copy.wait()
    total = dact_send[0].astype(jnp.float32)
    for by in range(1, samples):
        total = total + dact_in[by].astype(jnp.float32)
    total = total.astype(jnp.bfloat16).astype(jnp.float32)
    mid_rows[pl.ds(0, 32, stride=2), :] = total[:32]
    mid_rows[pl.ds(1, 32, stride=2), :] = total[32:]
    dpre_mid = (mid_rows[...] * leak_slope(pre_mid)).astype(jnp.bfloat16)
    back, dact_first = spread_back(dpre_mid, wide_mid, half[0] // 2, half[1] // 2, groups)
    back_send[...] = back.reshape(side, 128).astype(jnp.bfloat16)
    third = link(back_send, back_rim, ring, 2, at(0, -1))
    third.start()
    lax.fori_loop(1, chips, start_gather, 0)
    kept = pltpu.make_async_copy(block, blocks.at[chip, core], pair_sem.at[6])
    kept.start()
    row = 0
    for taps in taps_mid:
        data[row : row + 192] = contract_rows(taps, dpre_mid)[64:].astype(jnp.bfloat16)
        row += 192
    third.wait()
    edge = jnp.where(space < spaces - 1, back_rim[...].astype(jnp.float32), 0.0)
    flat = dact_first.reshape(-1, 128)
    flat = jnp.concatenate([flat[:-side], flat[-side:] + edge], axis=0)
    dpre_first = (flat * leak_slope(pre_first)).astype(jnp.bfloat16)
    for taps in taps_first:
        part = contract_rows(taps, dpre_first)
        part = part[96:192, :64] + part[160:256, 64:]
        part = jnp.concatenate([part[:48], part[48:]], axis=1)
        data[row : row + 48] = part.astype(jnp.bfloat16)
        row += 48
    data[row:] = jnp.zeros((data.shape[0] - row, 128), jnp.bfloat16)

    span = chips * rows_each

    def rows_at(side_of, slot):
        return pl.ds(pl.multiple_of(side_of * span + slot * rows_each, 16), rows_each)

    def pair_link(source, target, sems, step):
        return pltpu.make_async_remote_copy(
            src_ref=source,
            dst_ref=target,
            send_sem=sems.at[step],
            recv_sem=sems.at[chips + step],
            device_id=partner,
            device_id_type=MESH,
        )

    def halves(step):
        slot = lax.rem(chip + step, chips)
        return pair_link(data.at[rows_at(1 - core, slot)], half_in.at[step], half_sem, step)

    def start_halves(step, carry):
        halves(step).start()
        return carry

    lax.fori_loop(1, chips, start_halves, 0)
    halves(0).start()

    def own_half(step):
        halves(step).wait()
        rows = data[rows_at(core, lax.rem(chip + step, chips))].astype(jnp.float32)
        return rows + half_in[step].astype(jnp.float32)

    def scatter(step):
        to = lax.rem(chip + step, chips)
        return pltpu.make_async_remote_copy(
            src_ref=mine.at[step],
            dst_ref=parts.at[step],
            send_sem=send.at[step],
            recv_sem=recv.at[step],
            device_id=peer(to),
            device_id_type=MESH,
        )

    def start_scatter(step, carry):
        mine[step] = own_half(step).astype(jnp.bfloat16)
        scatter(step).start()
        return carry

    lax.fori_loop(1, chips, start_scatter, 0)
    kept.wait()
    lax.fori_loop(1, chips, wait_gather, 0)
    share = link(blocks.at[:, core], blocks.at[:, core], pair_sem, 1, partner)
    share.start()
    share.wait_send()
    link(blocks.at[:, 1 - core], blocks.at[:, 1 - core], pair_sem, 1, partner).wait_recv()


    chunk = min(spaces, 16)
    chunks = spaces // chunk
    grad_last[...] = jnp.zeros(grad_last.shape, jnp.float32)

    def contract_last(step, carry):
        start = (step // chunks) * pairs + lax.rem(step, chunks) * (chunk // 2)
        acts = blocks[pl.ds(start, chunk // 2)].astype(jnp.float32).reshape(chunk, BLOCK, 128)
        ahead = blocks[lax.max(start - 1, 0), 1].astype(jnp.float32)
        ahead = jnp.where(lax.rem(step, chunks) > 0, ahead, 0.0)
        before = jnp.concatenate([ahead[None], acts[:-1]], axis=0)
        grads_out = jnp.concatenate([acts[:, 64:72], acts[:, 72:80]], axis=2).reshape(chunk * 8, 256)
        grads_out = pick(grads_out).astype(jnp.bfloat16)
        for tap, rows in enumerate(last_taps(acts, before)):
            grad_last[tap] += contract_rows(rows, grads_out)
        return carry

    steps = samples * chunks
    lax.fori_loop(0, steps // 2, contract_last, 0)

    def collect(step, total):
        scatter(step).wait()
        return total + parts[step].astype(jnp.float32)

    done[...] = lax.fori_loop(1, chips, collect, own_half(0)).astype(jnp.bfloat16)

    def spread(step, slot):
        return pltpu.make_async_remote_copy(
            src_ref=done,
            dst_ref=result.at[rows_at(core, slot)],
            send_sem=send.at[chips + step],
            recv_sem=recv.at[chips + step],
            device_id=peer(lax.rem(chip + step, chips)),
            device_id_type=MESH,
        )

    def start_spread(step, carry):
        spread(step, chip).start()
        return carry

    def forward(source, side_of, step):
        slot = lax.rem(chip + chips - step, chips)
        return pair_link(source, result.at[rows_at(side_of, slot)], last_sem, step)

    def wait_spread(step, carry):
        slot = lax.rem(chip + chips - step, chips)
        spread(step, slot).wait()
        forward(result.at[rows_at(core, slot)], core, step).start()
        return carry

    def wait_forward(step, carry):
        slot = lax.rem(chip + chips - step, chips)
        forward(result.at[rows_at(core, slot)], core, step).wait_send()
        forward(result.at[rows_at(1 - core, slot)], 1 - core, step).wait_recv()
        return carry

    lax.fori_loop(1, chips, start_spread, 0)
    forward(done, core, 0).start()
    own = pltpu.make_async_copy(done, result.at[rows_at(core, chip)], pair_sem.at[7])
    own.start()

    here, behind = [], []
    earlier = lax.rem(space + spaces - 1, spaces)
    for by in range(samples):
        base = lax.rem(sample + by, samples) * pairs
        here.append(blocks[base + space // 2, core].astype(jnp.float32))
        behind.append(blocks[base + earlier // 2, lax.rem(earlier, 2)].astype(jnp.float32))
    behind = jnp.where(space > 0, jnp.stack(behind), 0.0)
    taps_last = last_taps(jnp.stack(here), behind)
    outputs = conv_taps(taps_last, weight_last).reshape(samples, 8, filters)
    out_send[...] = outputs
    out_copies = []
    for by in range(1, samples):
        out_copies.append(link(out_send.at[by], out_in.at[by], out_sem, by, at(by, 0)))
        out_copies[-1].start()

    lax.fori_loop(steps // 2, steps, contract_last, 0)
    for copy in out_copies:
        copy.wait()
    shards = []
    for shard in range(samples):
        value = out_send[0]
        for by in range(1, samples):
            value = jnp.where(lax.rem(sample + samples - by, samples) == shard, out_in[by], value)
        shards.append(value)
    shards = jnp.concatenate(shards, axis=1).astype(jnp.bfloat16)
    out_act[0] = shards[:4]
    out_act[1] = shards[4:]
    own.wait()
    lax.fori_loop(1, chips, wait_spread, 0)
    forward(done, core, 0).wait_send()
    forward(done, 1 - core, 0).wait_recv()
    lax.fori_loop(1, chips, wait_forward, 0)


def per_device(volume, cotangent, weight_first, weight_mid, weight_last):
    samples = lax.axis_size("sample")
    spaces = lax.axis_size("space")
    chips = samples * spaces // 2
    size_x, size_y, deep = volume.shape[1:]
    groups = deep // 128
    filters = weight_last.shape[4]
    edge = size_y * groups // 2
    count = 27 * 64 + 27 * 16
    rows_each = -(-count // (32 * chips)) * 16
    half = (chips * rows_each, 128)
    b16 = jnp.bfloat16
    dma = pltpu.SemaphoreType.DMA
    out_act, summed, grad_last = pl.pallas_call(
        functools.partial(whole_kernel, samples, spaces, (size_x, size_y, groups), rows_each),
        out_shape=[
            jax.ShapeDtypeStruct(cotangent.shape[2:], b16),
            jax.ShapeDtypeStruct((2 * half[0], 128), b16),
            jax.ShapeDtypeStruct((27, 128, filters), jnp.float32),
        ],
        in_specs=[VM] * 5,
        out_specs=[VM] * 3,
        scratch_shapes=[
            pltpu.VMEM((size_x * size_y * groups, 128), jnp.float32),
            pltpu.VMEM((size_y * groups, 128), jnp.float32),
            dma((2 * chips,)),
            dma((2 * chips,)),
            pltpu.VMEM((size_y, deep), b16),
            pltpu.VMEM((edge, 128), b16),
            pltpu.VMEM((edge, 128), b16),
            pltpu.VMEM((edge, 128), b16),
            pltpu.VMEM((edge, 128), b16),
            pltpu.VMEM((2, samples) + cotangent.shape[2:], b16),
            pltpu.VMEM((samples, 64, 128), b16),
            pltpu.VMEM((samples, 64, 128), b16),
            pltpu.VMEM((64, 128), jnp.float32),
            pltpu.VMEM((BLOCK, 128), b16),
            pltpu.VMEM((chips, 2, BLOCK, 128), b16),
            pltpu.VMEM((2 * half[0], 128), b16),
            pltpu.VMEM((chips, rows_each, 128), b16),
            pltpu.VMEM((chips, rows_each, 128), b16),
            pltpu.VMEM((chips, rows_each, 128), b16),
            pltpu.VMEM((rows_each, 128), b16),
            pltpu.VMEM((samples, 8, filters), jnp.float32),
            pltpu.VMEM((samples, 8, filters), jnp.float32),
            dma((6,)),
            dma((4 * samples,)),
            dma((2 * samples,)),
            dma((2 * chips,)),
            dma((2 * chips,)),
            dma((8,)),
            dma((chips,)),
            dma((chips,)),
            dma((2 * samples,)),
        ],
        compiler_params=pltpu.CompilerParams(collective_id=0, has_side_effects=True),
        name="whole",
    )(
        volume.reshape(-1, deep),
        cotangent.reshape(cotangent.shape[2:]),
        weight_first.reshape(27 * 32, 64),
        weight_mid.reshape(27 * 64, 128),
        weight_last.reshape(27, 128, filters),
    )
    rows_mid = 27 * 64
    grad_mid = summed[:rows_mid].astype(jnp.float32)
    tail = summed[rows_mid:count].astype(jnp.float32).reshape(9, 48, 128)
    grad_first = jnp.concatenate([tail[:, :, :64], tail[:, :, 64:]], axis=1)
    return (
        out_act.reshape(cotangent.shape),
        grad_first.reshape(weight_first.shape),
        grad_mid.reshape(weight_mid.shape),
        grad_last.reshape(weight_last.shape),
    )


def solution(mesh):
    in_specs = (
        P("sample", "space", None, None),
        P("sample", "space", None, None, None),
        P(),
        P(),
        P(None, None, None, None, "sample"),
    )
    out_specs = (
        P("sample", "space", None, None, None),
        P(),
        P(),
        P(None, None, None, None, "sample"),
    )
    return jax.shard_map(
        per_device, mesh=mesh, in_specs=in_specs, out_specs=out_specs, check_vma=False
    )
```

profile of v0, /device:TPU:0, one launch (start us, length us, event | category | flops | bytes accessed | tf_op | source)
XLA Modules:
  0.0 49.9 jit_solution(3956970379481450260)
XLA Ops:
  0.6 43.6 %whole.1 = (bf16[2,4,256]{2,1,0:T(4,128)(2,1)}, bf16[2560,128]{1,0:T(8,128)(2,1)}, f32[27,128,128]{2,1,0:T(8,128)}) custom-call(bf16[128,1024]{1,0:T(8,128)(2,1)} %bitcast.18, bf16[2,4,256]{2,1,0:T(4,128)(2,1)} %bitcast.20, bf16[864,64]{1,0:T(8,128)(2,1)} %bitcast.19, bf16[1728,128]{1,0:T(8,128)(2,1)} %bitcast.16, bf16[27,128,128]{2,1,0:T(8,128)(2,1)} %bitcast.15), custom_call_target="tpu_custom_call" | custom-call | tf_op jit(solution)/shard_map/whole/pallas_call | solution.py:501
  44.2 0.9 %slice.12 = bf16[432,128]{1,0:T(8,128)(2,1)S(1)} slice(bf16[2560,128]{1,0:T(8,128)(2,1)} %get-tuple-element.8), slice={[1728:2160], [0:128]} | slice | bytes 221184 | tf_op jit(solution)/shard_map/slice | solution.py:554
  45.1 1.0 %slice.15 = bf16[1728,128]{1,0:T(8,128)(2,1)S(1)} slice(bf16[2560,128]{1,0:T(8,128)(2,1)} %get-tuple-element.8), slice={[0:1728], [0:128]} | slice | bytes 884736 | tf_op jit(solution)/shard_map/slice | solution.py:553
  46.2 0.0 copy-start.1
  46.2 0.0 copy-start
  46.2 0.1 fusion
  46.3 0.8 %pad_maximum_fusion = f32[9,96,64]{2,1,0:T(8,128)} fusion(f32[9,48,64]{2,1,0:T(8,128)S(1)} %get-tuple-element.11, f32[9,48,64]{2,1,0:T(8,128)S(1)} %get-tuple-element.10), kind=kLoop, calls=%fused_computation | loop fusion | flops 55296 | bytes 442368 | tf_op jit(solution)/shard_map/concatenate | solution.py:555
  47.1 1.0 %convert.3 = f32[3,3,3,64,128]{4,3,2,1,0:T(8,128)} convert(bf16[3,3,3,64,128]{4,3,2,1,0:T(8,128)(2,1)S(1)} %bitcast.14) | non-fusion elementwise | flops 221184 | bytes 1327104 | tf_op jit(solution)/shard_map/reshape | solution.py:559
  48.1 0.0 copy-done.1
  48.1 0.6 %copy.11 = bf16[1,1,2,4,256]{4,3,2,1,0:T(4,128)(2,1)} copy(bf16[1,1,2,4,256]{4,3,2,1,0:T(4,128)(2,1)S(1)} %bitcast.21) | data formatting | bytes 8192
  48.7 0.0 copy-done
  48.7 1.2 %copy.12 = f32[3,3,3,128,128]{4,3,2,1,0:T(8,128)} copy(f32[3,3,3,128,128]{4,3,2,1,0:T(8,128)S(1)} %bitcast.13) | data formatting | bytes 3538944
Async XLA Ops:
  46.2 1.9 %copy-start.1 = (bf16[2,4,256]{2,1,0:T(4,128)(2,1)S(1)}, bf16[2,4,256]{2,1,0:T(4,128)(2,1)}, u32[]{:S(2)}) copy-start(bf16[2,4,256]{2,1,0:T(4,128)(2,1)} %get-tuple-element.7) | copy-start | bytes 12292
  46.2 2.5 %copy-start = (f32[27,128,128]{2,1,0:T(8,128)S(1)}, f32[27,128,128]{2,1,0:T(8,128)}, u32[]{:S(2)}) copy-start(f32[27,128,128]{2,1,0:T(8,128)} %get-tuple-element.9) | copy-start | bytes 5308420
where the time goes:
time: 50.1 us; the launch traced here: 49.9 us
  Pallas kernels  43.6 us (87%)
  local copies, waits for them, and re-layouts  3.85 us (8%)
  other arithmetic  1.81 us (4%)
  between operations  0.67 us (1%)
    pallas_call x1, Pallas kernels, per_device(): pl.pallas_call(functools.partial(whole_kernel, samples, spaces, (size_x,...  43.6 us
    unnamed x6, local copies, waits for them, and re-layouts  1.81 us
    slice x1, local copies, waits for them, and re-layouts, per_device(): grad_mid = summed[:rows_mid].astype(jnp.float32)  1.04 us
    reshape x1, other arithmetic, per_device(): grad_mid.reshape(weight_mid.shape)  1.01 us

commit v1 on v0

--- a/solution.py
+++ b/solution.py
@@ -485,6 +485,25 @@
     lax.fori_loop(1, chips, wait_forward, 0)
 
 
+def write_kernel(act, summed, last, out_act, grad_first, grad_mid, grad_last, first, mid, sems):
+    copies = [pltpu.make_async_copy(last, grad_last, sems.at[0])]
+    copies[-1].start()
+    copies.append(pltpu.make_async_copy(act, out_act, sems.at[1]))
+    copies[-1].start()
+    rows = mid.shape[0]
+    mid[...] = summed[:rows].astype(jnp.float32)
+    copies.append(pltpu.make_async_copy(mid, grad_mid, sems.at[2]))
+    copies[-1].start()
+    for tap in range(9):
+        tail = summed[rows + 48 * tap : rows + 48 * tap + 48].astype(jnp.float32)
+        first[96 * tap : 96 * tap + 48] = tail[:, :64]
+        first[96 * tap + 48 : 96 * tap + 96] = tail[:, 64:]
+    copies.append(pltpu.make_async_copy(first, grad_first, sems.at[3]))
+    copies[-1].start()
+    for copy in copies:
+        copy.wait()
+
+
 def per_device(volume, cotangent, weight_first, weight_mid, weight_last):
     samples = lax.axis_size("sample")
     spaces = lax.axis_size("space")
@@ -501,9 +520,9 @@
     out_act, summed, grad_last = pl.pallas_call(
         functools.partial(whole_kernel, samples, spaces, (size_x, size_y, groups), rows_each),
         out_shape=[
-            jax.ShapeDtypeStruct(cotangent.shape[2:], b16),
-            jax.ShapeDtypeStruct((2 * half[0], 128), b16),
-            jax.ShapeDtypeStruct((27, 128, filters), jnp.float32),
+            pltpu.VMEM(cotangent.shape[2:], b16),
+            pltpu.VMEM((2 * half[0], 128), b16),
+            pltpu.VMEM((27, 128, filters), jnp.float32),
         ],
         in_specs=[VM] * 5,
         out_specs=[VM] * 3,
@@ -540,7 +559,7 @@
             dma((chips,)),
             dma((2 * samples,)),
         ],
-        compiler_params=pltpu.CompilerParams(collective_id=0, has_side_effects=True),
+        compiler_params=pltpu.CompilerParams(collective_id=0, has_side_effects=True, vmem_limit_bytes=40 << 20),
         name="whole",
     )(
         volume.reshape(-1, deep),
@@ -549,10 +568,25 @@
         weight_mid.reshape(27 * 64, 128),
         weight_last.reshape(27, 128, filters),
     )
-    rows_mid = 27 * 64
-    grad_mid = summed[:rows_mid].astype(jnp.float32)
-    tail = summed[rows_mid:count].astype(jnp.float32).reshape(9, 48, 128)
-    grad_first = jnp.concatenate([tail[:, :, :64], tail[:, :, 64:]], axis=1)
+    any_spec = pl.BlockSpec(memory_space=pl.ANY)
+    out_act, grad_first, grad_mid, grad_last = pl.pallas_call(
+        write_kernel,
+        out_shape=[
+            jax.ShapeDtypeStruct(cotangent.shape[2:], b16),
+            jax.ShapeDtypeStruct((27 * 32, 64), jnp.float32),
+            jax.ShapeDtypeStruct((27 * 64, 128), jnp.float32),
+            jax.ShapeDtypeStruct((27, 128, filters), jnp.float32),
+        ],
+        in_specs=[VM] * 3,
+        out_specs=[any_spec] * 4,
+        scratch_shapes=[
+            pltpu.VMEM((27 * 32, 64), jnp.float32),
+            pltpu.VMEM((27 * 64, 128), jnp.float32),
+            dma((4,)),
+        ],
+        compiler_params=pltpu.CompilerParams(vmem_limit_bytes=16 << 20),
+        name="write",
+    )(*[pltpu.with_memory_space_constraint(value, pltpu.VMEM) for value in (out_act, summed, grad_last)])
     return (
         out_act.reshape(cotangent.shape),
         grad_first.reshape(weight_first.shape),

time: 50.1 us -> 48.2 us (0.962)
  other arithmetic: 1.81 us -> 0 us
  Pallas kernels: 43.6 us -> 42.5 us
  local copies, waits for them, and re-layouts: 3.85 us -> 4.74 us
    unnamed x6 -> x10, local copies, waits for them, and re-layouts: 1.81 us -> 4.74 us
    pallas_call x1, Pallas kernels: 43.6 us -> 40.8 us  [per_device(): pl.pallas_call(functools.partial(whole_kernel, samples, spaces, (size_x,...]
    slice x3 -> x0, local copies, waits for them, and re-layouts: 2.05 us -> none  [the longest x1 1.04 us: per_device(): grad_mid = summed[:rows_mid].astype(jnp.float32)]
    pallas_call x0 -> x1, Pallas kernels: none -> 1.68 us  [per_device(): pl.pallas_call(write_kernel, out_shape=[jax.ShapeDtypeStruct(cotangent.sh...]
    reshape x1 -> x0, other arithmetic: 1.01 us -> none  [per_device(): grad_mid.reshape(weight_mid.shape)]
    concatenate x1 -> x0, other arithmetic: 0.8 us -> none  [per_device(): grad_first = jnp.concatenate([tail[:, :, :64], tail[:, :, 64:]], axis=1)]
where the time goes in v1:
time: 48.2 us; the launch traced here: 47.9 us
  Pallas kernels  42.5 us (88%)
  local copies, waits for them, and re-layouts  4.74 us (10%)
  between operations  0.65 us (1%)
    pallas_call x1, Pallas kernels, per_device(): pl.pallas_call(functools.partial(whole_kernel, samples, spaces, (size_x,...  40.8 us
    unnamed x10, local copies, waits for them, and re-layouts  4.74 us
    pallas_call x1, Pallas kernels, per_device(): pl.pallas_call(write_kernel, out_shape=[jax.ShapeDtypeStruct(cotangent.sh...  1.68 us

profile of v1, /device:TPU:0, one launch (start us, length us, event | category | flops | bytes accessed | tf_op | source)
XLA Modules:
  0.0 47.9 jit_solution(990111361584018676)
XLA Ops:
  0.6 0.0 copy-start
  0.6 1.2 %copy-done = bf16[3,3,3,128,128]{4,3,2,1,0:T(8,128)(2,1)S(1)} copy-done((bf16[3,3,3,128,128]{4,3,2,1,0:T(8,128)(2,1)S(1)}, bf16[3,3,3,128,128]{4,3,2,1,0:T(8,128)(2,1)}, u32[]{:S(2)}) %copy-start) | copy-done | bytes 884760
  1.8 0.0 copy-start.1
  1.8 1.0 %copy-done.1 = bf16[3,3,3,64,128]{4,3,2,1,0:T(8,128)(2,1)S(1)} copy-done((bf16[3,3,3,64,128]{4,3,2,1,0:T(8,128)(2,1)S(1)}, bf16[3,3,3,64,128]{4,3,2,1,0:T(8,128)(2,1)}, u32[]{:S(2)}) %copy-start.1) | copy-done | bytes 442392
  2.8 0.0 copy-start.2
  2.8 0.9 %copy-done.2 = bf16[1,8,16,1024]{3,2,1,0:T(8,128)(2,1)S(1)} copy-done((bf16[1,8,16,1024]{3,2,1,0:T(8,128)(2,1)S(1)}, bf16[1,8,16,1024]{3,2,1,0:T(8,128)(2,1)}, u32[]{:S(2)}) %copy-start.2) | copy-done | bytes 262168
  3.8 0.0 copy-start.3
  3.8 0.9 %copy-done.3 = bf16[3,3,3,32,64]{4,3,2,1,0:T(8,128)(2,1)S(1)} copy-done((bf16[3,3,3,32,64]{4,3,2,1,0:T(8,128)(2,1)S(1)}, bf16[3,3,3,32,64]{4,3,2,1,0:T(8,128)(2,1)}, u32[]{:S(2)}) %copy-start.3) | copy-done | bytes 110616
  4.7 0.0 copy-start.4
  4.7 0.7 %copy-done.4 = bf16[1,1,2,4,256]{4,3,2,1,0:T(4,128)(2,1)S(1)} copy-done((bf16[1,1,2,4,256]{4,3,2,1,0:T(4,128)(2,1)S(1)}, bf16[1,1,2,4,256]{4,3,2,1,0:T(4,128)(2,1)}, u32[]{:S(2)}) %copy-start.4) | copy-done | bytes 4120
  5.4 40.8 %whole.1 = (bf16[2,4,256]{2,1,0:T(4,128)(2,1)S(1)}, bf16[2560,128]{1,0:T(8,128)(2,1)S(1)}, f32[27,128,128]{2,1,0:T(8,128)S(1)}) custom-call(bf16[128,1024]{1,0:T(8,128)(2,1)S(1)} %bitcast.11, bf16[2,4,256]{2,1,0:T(4,128)(2,1)S(1)} %bitcast.13, bf16[864,64]{1,0:T(8,128)(2,1)S(1)} %bitcast.12, bf16[1728,128]{1,0:T(8,128)(2,1)S(1)} %bitcast.10, ...), custom_call_target="tpu_custom_call" | custom-call | tf_op jit(solution)/shard_map/whole/pallas_call | solution.py:520
  46.2 1.7 %write.1 = (bf16[2,4,256]{2,1,0:T(4,128)(2,1)}, f32[864,64]{1,0:T(8,128)}, f32[1728,128]{1,0:T(8,128)}, f32[27,128,128]{2,1,0:T(8,128)}) custom-call(bf16[2,4,256]{2,1,0:T(4,128)(2,1)S(1)} %get-tuple-element.11.act, bf16[2560,128]{1,0:T(8,128)(2,1)S(1)} %get-tuple-element.12.summed, f32[27,128,128]{2,1,0:T(8,128)S(1)} %get-tuple-element.13.last), custom_call_target="tpu_custom_call" | custom-call | tf_op jit(solution)/shard_map/write/pallas_call | solution.py:572
Async XLA Ops:
  0.6 1.2 %copy-start = (bf16[3,3,3,128,128]{4,3,2,1,0:T(8,128)(2,1)S(1)}, bf16[3,3,3,128,128]{4,3,2,1,0:T(8,128)(2,1)}, u32[]{:S(2)}) copy-start(bf16[3,3,3,128,128]{4,3,2,1,0:T(8,128)(2,1)} %param.9) | copy-start | bytes 2654212
  1.8 1.0 %copy-start.1 = (bf16[3,3,3,64,128]{4,3,2,1,0:T(8,128)(2,1)S(1)}, bf16[3,3,3,64,128]{4,3,2,1,0:T(8,128)(2,1)}, u32[]{:S(2)}) copy-start(bf16[3,3,3,64,128]{4,3,2,1,0:T(8,128)(2,1)} %param.8) | copy-start | bytes 1327108
  2.8 0.9 %copy-start.2 = (bf16[1,8,16,1024]{3,2,1,0:T(8,128)(2,1)S(1)}, bf16[1,8,16,1024]{3,2,1,0:T(8,128)(2,1)}, u32[]{:S(2)}) copy-start(bf16[1,8,16,1024]{3,2,1,0:T(8,128)(2,1)} %param.5) | copy-start | bytes 786436
  3.8 0.9 %copy-start.3 = (bf16[3,3,3,32,64]{4,3,2,1,0:T(8,128)(2,1)S(1)}, bf16[3,3,3,32,64]{4,3,2,1,0:T(8,128)(2,1)}, u32[]{:S(2)}) copy-start(bf16[3,3,3,32,64]{4,3,2,1,0:T(8,128)(2,1)} %param.7) | copy-start | bytes 331780
  4.7 0.7 %copy-start.4 = (bf16[1,1,2,4,256]{4,3,2,1,0:T(4,128)(2,1)S(1)}, bf16[1,1,2,4,256]{4,3,2,1,0:T(4,128)(2,1)}, u32[]{:S(2)}) copy-start(bf16[1,1,2,4,256]{4,3,2,1,0:T(4,128)(2,1)} %param.6) | copy-start | bytes 12292
